TPU v7x, 32 devices: a whole 2x2x4 slice. The times are simulated.
32 devices in a mesh: dev: 32 (over z, y, x, core).
Axes of the slice: x: 2, y: 2, z: 4, core: 2. Of those that a mesh axis runs over, the one named last changes fastest.
Arguments:
- tokens: bfloat16 [32768, 384], P('dev'), may hold values from -6 to 6
- image_ids: int32 [32768], replicated, may hold values from 0 to 220, never falling along the last dimension, each value on 1 to 197 neighbouring positions
- cotangent: bfloat16 [32768, 384], P('dev'), may hold values from -6 to 6
- w_qkv: bfloat16 [2, 384, 1152], P(None, 'dev'), may hold values from -0.3125 to 0.3125
- bias_qv: bfloat16 [2, 768], P(None, 'dev'), may hold values from -3 to 3
- w_out: bfloat16 [2, 384, 384], P(None, 'dev'), may hold values from -1.25 to 1.25
- bias_out: bfloat16 [2, 384], P(None, 'dev'), may hold values from -3 to 3
- w_up: bfloat16 [2, 384, 1536], P(None, 'dev'), may hold values from -0.3125 to 0.3125
- bias_up: bfloat16 [2, 1536], P(None, 'dev'), may hold values from -3 to 3
- w_down: bfloat16 [2, 1536, 384], P(None, 'dev'), may hold values from -0.15625 to 0.15625
- bias_down: bfloat16 [2, 384], P(None, 'dev'), may hold values from -3 to 3
- norm1_gain: bfloat16 [2, 384], P(None, 'dev'), may hold values from 0.5 to 1.5
- norm1_shift: bfloat16 [2, 384], P(None, 'dev'), may hold values from -1.75 to 1.75
- norm2_gain: bfloat16 [2, 384], P(None, 'dev'), may hold values from 0.5 to 1.5
- norm2_shift: bfloat16 [2, 384], P(None, 'dev'), may hold values from -1.75 to 1.75
Outputs:
- output: bfloat16 [32768, 384], P('dev')
- grad_tokens: float32 [32768, 384], P('dev')
- grad_w_qkv: float32 [2, 384, 1152], P(None, 'dev')
- grad_bias_qv: float32 [2, 768], P(None, 'dev')
- grad_w_out: float32 [2, 384, 384], P(None, 'dev')
- grad_bias_out: float32 [2, 384], P(None, 'dev')
- grad_w_up: float32 [2, 384, 1536], P(None, 'dev')
- grad_bias_up: float32 [2, 1536], P(None, 'dev')
- grad_w_down: float32 [2, 1536, 384], P(None, 'dev')
- grad_bias_down: float32 [2, 384], P(None, 'dev')
- grad_norm1_gain: float32 [2, 384], P(None, 'dev')
- grad_norm1_shift: float32 [2, 384], P(None, 'dev')
- grad_norm2_gain: float32 [2, 384], P(None, 'dev')
- grad_norm2_shift: float32 [2, 384], P(None, 'dev')
Inputs may be any that keep to these rules, and one draw needn't show every extreme that they name: `image_ids`: image ids never fall along the tokens, so each image is a run of consecutive tokens; every image holds 1 to 197 tokens and one holds exactly 197.
All inputs are finite; a program needn't handle non-finite values.
Results may differ from a plain program's by a relative error of at most 0.012.
Values may be sent and summed in bfloat16 or wider, within the bound.
No kernel may reach another device: no remote copies, remote signals or barrier semaphores. Data moves between devices by JAX's collectives and lax.ppermute only.
A program may use at most 192 MiB of HBM per device.

v0:
```python
import jax
import jax.numpy as jnp
from jax import lax
from jax.sharding import PartitionSpec as P

HEADS = 6
HEAD_DIM = 64
LAYERS = 2
HALO = 256
QB = 512
SCALE = 0.125
NEGATIVE = -1e30
EPSILON = 1e-06


def passed_along(value, axis, steps):
    count = lax.axis_size(axis)
    leading, last = (max(0, -steps), min(count, count - steps))
    return lax.ppermute(value, axis, [(source, source + steps) for source in range(leading, last)])


def padded(block, sides, width):
    for axis, dim in sides:
        count = lax.axis_size(axis)
        forward = [(i, i + 1) for i in range(count - 1)]
        backward = [(target, source) for source, target in forward]
        low = lax.ppermute(
            lax.slice_in_dim(block, block.shape[dim] - width, None, axis=dim), axis, forward
        )
        high = lax.ppermute(lax.slice_in_dim(block, 0, width, axis=dim), axis, backward)
        block = jnp.concatenate([low, block, high], axis=dim)
    return block


def layer_norm(values, gain, shift):
    centre = jnp.mean(values, axis=-1, keepdims=True)
    centred = values - centre
    spread = jnp.mean(centred * centred, axis=-1, keepdims=True)
    return centred * lax.rsqrt(spread + EPSILON) * gain + shift


def product(left, right):
    return jnp.dot(left, right, preferred_element_type=jnp.float32)


def contract_rows(left, right):
    return lax.dot_general(
        left, right, (((0,), (0,)), ((), ())), preferred_element_type=jnp.float32
    )


def contract_last(left, right):
    return lax.dot_general(
        left, right, (((1,), (1,)), ((), ())), preferred_element_type=jnp.float32
    )


def gelu_exact(values):
    return jax.nn.gelu(values, approximate=False)


def fetch_forward(shards):
    return (
        lax.all_gather(shards[0], "dev", axis=0, tiled=True),
        lax.all_gather(shards[1], "dev", axis=0, tiled=True),
        lax.all_gather(shards[2], "dev", axis=0, tiled=True),
        lax.all_gather(shards[3], "dev", axis=0, tiled=True),
        lax.all_gather(shards[4], "dev", axis=0, tiled=True),
        lax.all_gather(shards[5], "dev", axis=0, tiled=True),
        lax.all_gather(shards[6], "dev", axis=0, tiled=True),
        lax.all_gather(shards[7], "dev", axis=0, tiled=True),
        lax.all_gather(shards[8], "dev", axis=0, tiled=True),
        lax.all_gather(shards[9], "dev", axis=0, tiled=True),
        lax.all_gather(shards[10], "dev", axis=0, tiled=True),
        lax.all_gather(shards[11], "dev", axis=0, tiled=True),
    )


def fetch_backward(shards):
    return (
        lax.all_gather(shards[0], "dev", axis=0, tiled=True),
        lax.all_gather(shards[1], "dev", axis=0, tiled=True),
        lax.all_gather(shards[2], "dev", axis=0, tiled=True),
        lax.all_gather(shards[3], "dev", axis=0, tiled=True),
        lax.all_gather(shards[4], "dev", axis=0, tiled=True),
        lax.all_gather(shards[5], "dev", axis=0, tiled=True),
        lax.all_gather(shards[6], "dev", axis=0, tiled=True),
        lax.all_gather(shards[7], "dev", axis=0, tiled=True),
        lax.all_gather(shards[8], "dev", axis=0, tiled=True),
        lax.all_gather(shards[9], "dev", axis=0, tiled=True),
        lax.all_gather(shards[10], "dev", axis=0, tiled=True),
        lax.all_gather(shards[11], "dev", axis=0, tiled=True),
    )


def reduce_layer(terms):
    return (
        lax.psum_scatter(terms[0], "dev", scatter_dimension=0, tiled=True),
        lax.psum_scatter(terms[1], "dev", scatter_dimension=0, tiled=True),
        lax.psum_scatter(terms[2], "dev", scatter_dimension=0, tiled=True),
        lax.psum_scatter(terms[3], "dev", scatter_dimension=0, tiled=True),
        lax.psum_scatter(terms[4], "dev", scatter_dimension=0, tiled=True),
        lax.psum_scatter(terms[5], "dev", scatter_dimension=0, tiled=True),
        lax.psum_scatter(terms[6], "dev", scatter_dimension=0, tiled=True),
        lax.psum_scatter(terms[7], "dev", scatter_dimension=0, tiled=True),
        lax.psum_scatter(terms[8], "dev", scatter_dimension=0, tiled=True),
        lax.psum_scatter(terms[9], "dev", scatter_dimension=0, tiled=True),
        lax.psum_scatter(terms[10], "dev", scatter_dimension=0, tiled=True),
        lax.psum_scatter(terms[11], "dev", scatter_dimension=0, tiled=True),
    )


def block_scores(queries, keys_values, id_query, id_keys, first):
    width = queries.shape[1]
    window = QB + 2 * HALO
    query_block = lax.dynamic_slice_in_dim(queries, first, QB, 0).reshape(QB, HEADS, HEAD_DIM)
    key_window = lax.dynamic_slice_in_dim(keys_values, first, window, 0)
    key_heads = key_window[:, :width].reshape(window, HEADS, HEAD_DIM)
    value_heads = key_window[:, width:].reshape(window, HEADS, HEAD_DIM)
    query_ids = lax.dynamic_slice_in_dim(id_query, first, QB, 0)
    window_ids = lax.dynamic_slice_in_dim(id_keys, first, window, 0)
    same_image = query_ids[:, None] == window_ids[None, :]
    scores = (
        jnp.einsum("qhd,khd->hqk", query_block, key_heads, preferred_element_type=jnp.float32)
        * SCALE
    )
    scores = jnp.where(same_image[None], scores, NEGATIVE)
    return (query_block, key_heads, value_heads, scores)


def attend(queries, keys_values, id_query, id_keys):
    row_count, width = queries.shape

    def one_block(block_no):
        first = block_no * QB
        query_block, key_heads, value_heads, scores = block_scores(
            queries, keys_values, id_query, id_keys, first
        )
        highest = jnp.max(scores, axis=2, keepdims=True)
        exponent_terms = jnp.exp(scores - highest)
        totals = jnp.sum(exponent_terms, axis=2, keepdims=True)
        soft_low = (exponent_terms / totals).astype(jnp.bfloat16)
        attended = jnp.einsum(
            "hqk,khd->qhd", soft_low, value_heads, preferred_element_type=jnp.float32
        )
        return (
            attended.reshape(QB, width).astype(jnp.bfloat16),
            (highest + jnp.log(totals))[:, :, 0],
        )

    attended, log_totals = lax.map(one_block, jnp.arange(row_count // QB, dtype=jnp.int32))
    return (attended.reshape(row_count, width), log_totals)


def attend_back(queries, keys_values, id_query, id_keys, log_totals, grad_attended):
    row_count, width = queries.shape
    window = QB + 2 * HALO

    def one_block(block_no, carry):
        grad_queries, grad_window = carry
        first = block_no * QB
        query_block, key_heads, value_heads, scores = block_scores(
            queries, keys_values, id_query, id_keys, first
        )
        soft = jnp.exp(scores - log_totals[block_no][:, :, None])
        grad_block = lax.dynamic_slice_in_dim(grad_attended, first, QB, 0).reshape(
            QB, HEADS, HEAD_DIM
        )
        grad_soft = jnp.einsum(
            "qhd,khd->hqk", grad_block, value_heads, preferred_element_type=jnp.float32
        )
        inner = jnp.sum(soft * grad_soft, axis=2, keepdims=True)
        grad_scores = (soft * (grad_soft - inner)).astype(jnp.bfloat16)
        block_queries = (
            jnp.einsum(
                "hqk,khd->qhd", grad_scores, key_heads, preferred_element_type=jnp.float32
            ).reshape(QB, width)
            * SCALE
        )
        block_keys = (
            jnp.einsum(
                "hqk,qhd->khd", grad_scores, query_block, preferred_element_type=jnp.float32
            ).reshape(window, width)
            * SCALE
        )
        block_values = jnp.einsum(
            "hqk,qhd->khd",
            soft.astype(jnp.bfloat16),
            grad_block,
            preferred_element_type=jnp.float32,
        ).reshape(window, width)
        grad_queries = lax.dynamic_update_slice_in_dim(grad_queries, block_queries, first, 0)
        previous = lax.dynamic_slice_in_dim(grad_window, first, window, 0)
        grad_window = lax.dynamic_update_slice_in_dim(
            grad_window, previous + jnp.concatenate([block_keys, block_values], axis=1), first, 0
        )
        return (grad_queries, grad_window)

    start_carry = (
        jnp.zeros((row_count, width), jnp.float32),
        jnp.zeros((row_count + 2 * HALO, 2 * width), jnp.float32),
    )
    grad_queries, grad_window = lax.fori_loop(0, row_count // QB, one_block, start_carry)
    from_next = passed_along(grad_window[:HALO].astype(jnp.bfloat16), "dev", -1).astype(jnp.float32)
    from_prior = passed_along(
        grad_window[row_count + HALO :].astype(jnp.bfloat16), "dev", 1
    ).astype(jnp.float32)
    grad_own = grad_window[HALO : HALO + row_count]
    grad_own = grad_own.at[row_count - HALO :].add(from_next)
    grad_own = grad_own.at[:HALO].add(from_prior)
    return (grad_queries, grad_own)


def forward_layer(stream, weights_full, id_query, id_keys):
    (
        w_qkv,
        bias_qv,
        w_out,
        bias_out,
        w_up,
        bias_up,
        w_down,
        bias_down,
        gain_one,
        shift_one,
        gain_two,
        shift_two,
    ) = weights_full
    width = stream.shape[1]
    normed = layer_norm(stream, gain_one.astype(jnp.float32), shift_one.astype(jnp.float32)).astype(
        jnp.bfloat16
    )
    mixed = product(normed, w_qkv)
    bias_float = bias_qv.astype(jnp.float32)
    queries = (mixed[:, :width] + bias_float[:width]).astype(jnp.bfloat16)
    keys_values = jnp.concatenate(
        [mixed[:, width : 2 * width], mixed[:, 2 * width :] + bias_float[width:]], axis=1
    ).astype(jnp.bfloat16)
    rim_keys = padded(keys_values, (("dev", 0),), HALO)
    attended, log_totals = attend(queries, rim_keys, id_query, id_keys)
    after = stream + product(attended, w_out) + bias_out.astype(jnp.float32)
    normed_two = layer_norm(
        after, gain_two.astype(jnp.float32), shift_two.astype(jnp.float32)
    ).astype(jnp.bfloat16)
    pre_hidden = product(normed_two, w_up) + bias_up.astype(jnp.float32)
    hidden = gelu_exact(pre_hidden).astype(jnp.bfloat16)
    result = after + product(hidden, w_down) + bias_down.astype(jnp.float32)
    saved = (
        stream,
        normed,
        queries,
        rim_keys,
        attended,
        log_totals,
        after,
        normed_two,
        pre_hidden,
        hidden,
    )
    return (result, saved)


def backward_layer(grad_stream, saved, weights_full, id_query, id_keys):
    (
        stream,
        normed,
        queries,
        rim_keys,
        attended,
        log_totals,
        after,
        normed_two,
        pre_hidden,
        hidden,
    ) = saved
    (
        w_qkv,
        bias_qv,
        w_out,
        bias_out,
        w_up,
        bias_up,
        w_down,
        bias_down,
        gain_one,
        shift_one,
        gain_two,
        shift_two,
    ) = weights_full
    width = stream.shape[1]
    grad_branch = grad_stream.astype(jnp.bfloat16)
    grad_w_down = contract_rows(hidden, grad_branch)
    grad_bias_down = jnp.sum(grad_branch.astype(jnp.float32), axis=0)
    grad_hidden = contract_last(grad_branch, w_down)
    unused_gelu, gelu_pull = jax.vjp(gelu_exact, pre_hidden)
    grad_pre = gelu_pull(grad_hidden)[0].astype(jnp.bfloat16)
    grad_w_up = contract_rows(normed_two, grad_pre)
    grad_bias_up = jnp.sum(grad_pre.astype(jnp.float32), axis=0)
    grad_normed_two = contract_last(grad_pre, w_up)
    unused_two, norm_two_pull = jax.vjp(
        layer_norm, after, gain_two.astype(jnp.float32), shift_two.astype(jnp.float32)
    )
    grad_norm_after, grad_gain_two, grad_shift_two = norm_two_pull(grad_normed_two)
    grad_after = grad_stream + grad_norm_after
    grad_out_branch = grad_after.astype(jnp.bfloat16)
    grad_w_out = contract_rows(attended, grad_out_branch)
    grad_bias_out = jnp.sum(grad_out_branch.astype(jnp.float32), axis=0)
    grad_attended = contract_last(grad_out_branch, w_out).astype(jnp.bfloat16)
    grad_queries, grad_keys_values = attend_back(
        queries, rim_keys, id_query, id_keys, log_totals, grad_attended
    )
    grad_mixed = jnp.concatenate([grad_queries, grad_keys_values], axis=1).astype(jnp.bfloat16)
    grad_w_qkv = contract_rows(normed, grad_mixed)
    mixed_sums = jnp.sum(grad_mixed.astype(jnp.float32), axis=0)
    grad_bias_qv = jnp.concatenate([mixed_sums[:width], mixed_sums[2 * width :]])
    grad_normed = contract_last(grad_mixed, w_qkv)
    unused_one, norm_one_pull = jax.vjp(
        layer_norm, stream, gain_one.astype(jnp.float32), shift_one.astype(jnp.float32)
    )
    grad_norm_stream, grad_gain_one, grad_shift_one = norm_one_pull(grad_normed)
    gradients = (
        grad_w_qkv,
        grad_bias_qv,
        grad_w_out,
        grad_bias_out,
        grad_w_up,
        grad_bias_up,
        grad_w_down,
        grad_bias_down,
        grad_gain_one,
        grad_shift_one,
        grad_gain_two,
        grad_shift_two,
    )
    return (grad_after + grad_norm_stream, gradients)


def on_device(
    tokens,
    image_ids,
    cotangent,
    w_qkv,
    bias_qv,
    w_out,
    bias_out,
    w_up,
    bias_up,
    w_down,
    bias_down,
    norm1_gain,
    norm1_shift,
    norm2_gain,
    norm2_shift,
):
    row_count = tokens.shape[0]
    first_row = lax.axis_index("dev") * row_count
    rim_ids = jnp.full((HALO,), -1, jnp.int32)
    padded_ids = jnp.concatenate([rim_ids, image_ids, rim_ids])
    id_query = lax.dynamic_slice_in_dim(image_ids, first_row, row_count, 0)
    id_keys = lax.dynamic_slice_in_dim(padded_ids, first_row, row_count + 2 * HALO, 0)
    shards = (
        w_qkv,
        bias_qv,
        w_out,
        bias_out,
        w_up,
        bias_up,
        w_down,
        bias_down,
        norm1_gain,
        norm1_shift,
        norm2_gain,
        norm2_shift,
    )
    stream = tokens.astype(jnp.float32)
    saved_all = []
    weights_all = []
    for layer_no in range(LAYERS):
        weights_full = fetch_forward(tuple((piece[layer_no] for piece in shards)))
        stream, saved = forward_layer(stream, weights_full, id_query, id_keys)
        saved_all.append(saved)
        weights_all.append(weights_full)
    final = stream.astype(jnp.bfloat16)
    grad_stream = cotangent.astype(jnp.float32)
    layer_terms = [None] * LAYERS
    for layer_no in range(LAYERS - 1, -1, -1):
        weights_full = fetch_backward(tuple((piece[layer_no] for piece in shards)))
        grad_stream, gradients = backward_layer(
            grad_stream, saved_all[layer_no], weights_full, id_query, id_keys
        )
        layer_terms[layer_no] = reduce_layer(gradients)
    owned = tuple(
        (
            jnp.stack([layer_terms[layer_no][member] for layer_no in range(LAYERS)])
            for member in range(12)
        )
    )
    return (
        final,
        grad_stream,
        owned[0],
        owned[1],
        owned[2],
        owned[3],
        owned[4],
        owned[5],
        owned[6],
        owned[7],
        owned[8],
        owned[9],
        owned[10],
        owned[11],
    )


def solution(mesh):
    in_specs = (
        P("dev", None),
        P(),
        P("dev", None),
        P(None, "dev", None),
        P(None, "dev"),
        P(None, "dev", None),
        P(None, "dev"),
        P(None, "dev", None),
        P(None, "dev"),
        P(None, "dev", None),
        P(None, "dev"),
        P(None, "dev"),
        P(None, "dev"),
        P(None, "dev"),
        P(None, "dev"),
    )
    out_specs = (
        P("dev", None),
        P("dev", None),
        P(None, "dev", None),
        P(None, "dev"),
        P(None, "dev", None),
        P(None, "dev"),
        P(None, "dev", None),
        P(None, "dev"),
        P(None, "dev", None),
        P(None, "dev"),
        P(None, "dev"),
        P(None, "dev"),
        P(None, "dev"),
        P(None, "dev"),
    )
    return jax.shard_map(
        on_device, mesh=mesh, in_specs=in_specs, out_specs=out_specs, check_vma=False
    )
```

profile of v0, /device:TPU:4, one launch (start us, length us, event | category | flops | bytes accessed | tf_op | source)
XLA Modules:
  0.0 997.2 jit_solution(3221153237229773106)
XLA Ops:
  21.5 42.1 %all-reduce.45 = (bf16[768]{0:T(1024)(128)(2,1)S(1)}, bf16[768]{0:T(1024)(128)(2,1)S(1)}, bf16[384]{0:T(512)(128)(2,1)S(1)}, bf16[384]{0:T(512)(128)(2,1)S(1)}, ...) all-reduce(bf16[768]{0:T(1024)(128)(2,1)S(1)} %dynamic-update-slice, ...), channel_id=5, replica_groups=mesh['dev'=32] {'dev'}, use_global_device_ids=true, to_apply=%add.2 | all-reduce | flops 9216 | bytes 36864
  64.6 41.3 %all-gather.2 = bf16[1,384,1152]{2,0,1:T(2,128)(2,1)S(1)} all-gather(bf16[1,12,1152]{2,0,1:T(2,128)(2,1)S(1)} %get-tuple-element.782), channel_id=4, replica_groups=mesh['dev'=32] {'dev'}, dimensions={1}, use_global_device_ids=true | all-gather | bytes 912384 | tf_op jit(solution)/shard_map/all_gather | solution.py:64
  120.4 41.0 %all-gather.4 = bf16[1,384,384]{2,0,1:T(2,128)(2,1)} all-gather(bf16[1,12,384]{2,0,1:T(2,128)(2,1)S(1)} %get-tuple-element.784), channel_id=6, replica_groups=mesh['dev'=32] {'dev'}, dimensions={1}, use_global_device_ids=true | all-gather | bytes 304128 | tf_op jit(solution)/shard_map/all_gather | solution.py:66
  162.6 46.1 %all-gather.14 = bf16[1,384,1152]{2,0,1:T(2,128)(2,1)} all-gather(bf16[1,12,1152]{2,0,1:T(2,128)(2,1)S(1)} %get-tuple-element.781), channel_id=16, replica_groups=mesh['dev'=32] {'dev'}, dimensions={1}, use_global_device_ids=true | all-gather | bytes 912384 | tf_op jit(solution)/shard_map/all_gather | solution.py:64
  216.6 34.5 %while.58 = (s32[]{:T(128)}, bf16[2,512,384]{2,1,0:T(8,128)(2,1)}, f32[2,6,512]{2,1,0:T(8,128)}, s32[2]{0:T(128)}, bf16[1536,768]{0,1:T(8,128)(2,1)S(1)}, /*inde...) while((s32[]{:T(128)}, bf16[2,512,384]{2,1,0:T(8,128)(2,1)}, ...), condition=%wide.region_5.6_spmd, body=%wide.region_2.5_spmd.sunk | while | flops 843772928 | bytes 47831304 | solution.py:151
  255.4 31.3 %multiply_convert_fusion.3 = (bf16[1024,1536]{1,0:T(8,128)(2,1)}, f32[1024,1536]{1,0:T(8,128)}, f32[1024,1536]{1,0:T(8,128)}) fusion(f32[1536]{0:T(1024)S(1)} %copy-done.112, bf16[1,384,1536]{2,0,1:T(2,128)(2,1)} %all-gather.29.cloned.1.call-done, f32[1024,384]{0,1:T(8,128)} %copy-done.11, f32[384]{0:T(512)S(1)} %copy-done.122, ...), kind=kOutput, calls=%fused_computation.85 | convolution fusion | flops 1313734656 | bytes 18498560 | tf_op jit(solution)/shard_map/dot_general | solution.py:43
  306.1 39.2 %all-gather.16 = bf16[1,384,384]{2,0,1:T(2,128)(2,1)} all-gather(bf16[1,12,384]{2,0,1:T(2,128)(2,1)S(1)} %copy-done.77), channel_id=18, replica_groups=mesh['dev'=32] {'dev'}, dimensions={1}, use_global_device_ids=true | all-gather | bytes 304128 | tf_op jit(solution)/shard_map/all_gather | solution.py:66
  353.2 32.5 %while.59 = (s32[]{:T(128)}, bf16[2,512,384]{2,1,0:T(8,128)(2,1)}, f32[2,6,512]{2,1,0:T(8,128)}, s32[2]{0:T(128)}, bf16[1536,768]{0,1:T(8,128)(2,1)S(1)}, /*inde...) while((s32[]{:T(128)}, bf16[2,512,384]{2,1,0:T(8,128)(2,1)}, ...), condition=%wide.region_13.14_spmd, body=%wide.region_10.13_spmd.sunk | while | flops 843772928 | bytes 47831304 | solution.py:151
  389.6 20.0 %multiply_convert_fusion.2 = (bf16[1024,1536]{1,0:T(8,128)(2,1)}, f32[1024,1536]{1,0:T(8,128)}, f32[1024,1536]{1,0:T(8,128)}) fusion(f32[1536]{0:T(1024)S(1)} %copy-done.114, bf16[1,384,1536]{2,0,1:T(2,128)(2,1)} %all-gather.33.cloned.1.call-done, f32[1024,384]{0,1:T(8,128)} %copy-done.14, f32[384]{0:T(512)S(1)} %copy-done.126, ...), kind=kOutput, calls=%fused_computation.72 | convolution fusion | flops 1313734656 | bytes 18498560 | tf_op jit(solution)/shard_map/dot_general | solution.py:43
  409.6 9.5 convert_reduce_fusion
  439.2 63.3 %while.60 = (s32[]{:T(128)}, bf16[1024,384]{0,1:T(8,128)(2,1)}, f32[1536,768]{0,1:T(8,128)}, bf16[1536,768]{0,1:T(8,128)(2,1)S(1)}, s32[1024]{0:T(1024)S(1)}, /*...) while((s32[]{:T(128)}, bf16[1024,384]{0,1:T(8,128)(2,1)}, ...), condition=%wide.region_20.21_spmd, body=%wide.region_18.20_spmd.sunk | while | flops 2063332352 | bytes 165468752 | solution.py:203
  450.2 7.1 multiply_reduce_fusion.13
  457.3 6.9 multiply_convert_fusion.6
  481.5 7.1 multiply_reduce_fusion.13
  488.7 6.9 multiply_convert_fusion.6
  506.1 5.7 collective-permute-start.4
  537.6 8.1 convert_reduce_fusion.1
  559.4 61.0 %while.61 = (s32[]{:T(128)}, bf16[1024,384]{0,1:T(8,128)(2,1)}, f32[1536,768]{0,1:T(8,128)}, bf16[1536,768]{0,1:T(8,128)(2,1)S(1)}, s32[1024]{0:T(1024)S(1)}, /*...) while((s32[]{:T(128)}, bf16[1024,384]{0,1:T(8,128)(2,1)}, ...), condition=%wide.region_27.28_spmd, body=%wide.region_25.27_spmd.sunk | while | flops 2063332352 | bytes 165468752 | solution.py:203
  569.3 7.2 multiply_reduce_fusion.14
  576.5 6.9 multiply_convert_fusion.7
  599.6 7.1 multiply_reduce_fusion.14
  606.8 6.9 multiply_convert_fusion.7
  660.7 145.1 %fusion.121 = (f32[16,1152]{1,0:T(8,128)S(1)}, f32[16,1152]{1,0:T(8,128)S(1)}, f32[16,384]{1,0:T(8,128)S(1)}, f32[16,384]{1,0:T(8,128)S(1)}, f32[16,1536]{1,0:T(8,128)S(1)}, /*index=5*/f32[16,1536]{1,0:T(8,128)S(1)}) fusion(f32[384,1152]{1,0:T(8,128)} %fusion.84, f32[384,1152]{1,0:T(8,128)} %fusion.83, f32[384,384]{1,0:T(8,128)S(1)} %copy-done.50, ...), kind=kCustom, calls=%all-reduce-scatter.6 | all-reduce-scatter fusion | flops 3145729 | bytes 9830400
  818.4 39.4 %all-reduce.44 = (f32[768]{0:T(1024)S(1)}, f32[768]{0:T(1024)S(1)}, f32[384]{0:T(512)S(1)}, f32[384]{0:T(512)S(1)}, f32[1536]{0:T(1024)S(1)}, /*index=5*/f32[153...) all-reduce(f32[768]{0:T(1024)S(1)} %pad_maximum_fusion.17, ...), channel_id=29, replica_groups=mesh['dev'=32] {'dev'}, use_global_device_ids=true, to_apply=%region_35.36.clone | all-reduce | flops 9216 | bytes 73728
  (778 shorter events, 450.4 us)
Async XLA Ops:
  7.2 248.1 %all-gather.29.cloned.1.call-start = ((), (), s32[]{:S(2)}) async-start(), calls=%async_computation.4 | async-start | bytes 2433024 | tf_op jit(solution)/shard_map/all_gather | solution.py:68
  9.0 277.7 %all-gather.31.cloned.1.call-start = ((), (), s32[]{:S(2)}) async-start(), calls=%async_computation.5 | async-start | bytes 1216512 | tf_op jit(solution)/shard_map/all_gather | solution.py:70
  10.5 379.0 %all-gather.33.cloned.1.call-start = ((), (), s32[]{:S(2)}) async-start(), calls=%async_computation.6 | async-start | bytes 2433024 | tf_op jit(solution)/shard_map/all_gather | solution.py:68
  109.1 99.7 %collective-permute-start = (bf16[256,768]{1,0:T(8,128)(2,1)}, bf16[256,768]{1,0:T(8,128)(2,1)}, u32[]{:S(2)}, u32[]{:S(2)}) collective-permute-start(bf16[256,768]{1,0:T(8,128)(2,1)} %get-tuple-element.774), channel_id=1, source_target_pairs={{0,1},{1,2},{2,3},{3,4},{4,5},{5,6},{6,7},{7,8},{8,9},{9,10},{10,1... | collective-permute-start | bytes 1179656 | tf_op jit(solution)/shard_map/ppermute | solution.py:27
  111.3 97.5 %collective-permute-start.1 = (bf16[256,768]{1,0:T(8,128)(2,1)}, bf16[256,768]{1,0:T(8,128)(2,1)}, u32[]{:S(2)}, u32[]{:S(2)}) collective-permute-start(bf16[256,768]{1,0:T(8,128)(2,1)} %get-tuple-element.775), channel_id=1, source_target_pairs={{1,0},{2,1},{3,2},{4,3},{5,4},{6,5},{7,6},{8,7},{9,8},{10,9},{11,1... | collective-permute-start | bytes 1179656 | tf_op jit(solution)/shard_map/ppermute | solution.py:30
  115.5 294.0 %all-gather.35.cloned.1.call-start = ((), (), s32[]{:S(2)}) async-start(), calls=%async_computation.7 | async-start | bytes 1216512 | tf_op jit(solution)/shard_map/all_gather | solution.py:70
  294.5 51.0 %collective-permute-start.2 = (bf16[256,768]{1,0:T(8,128)(2,1)}, bf16[256,768]{1,0:T(8,128)(2,1)}, u32[]{:S(2)}, u32[]{:S(2)}) collective-permute-start(bf16[256,768]{1,0:T(8,128)(2,1)} %get-tuple-element.772), channel_id=1, source_target_pairs={{0,1},{1,2},{2,3},{3,4},{4,5},{5,6},{6,7},{7,8},{8,9},{9,10},{10,1... | collective-permute-start | bytes 1179656 | tf_op jit(solution)/shard_map/ppermute | solution.py:27
  296.8 48.8 %collective-permute-start.3 = (bf16[256,768]{1,0:T(8,128)(2,1)}, bf16[256,768]{1,0:T(8,128)(2,1)}, u32[]{:S(2)}, u32[]{:S(2)}) collective-permute-start(bf16[256,768]{1,0:T(8,128)(2,1)} %get-tuple-element.773), channel_id=1, source_target_pairs={{1,0},{2,1},{3,2},{4,3},{5,4},{6,5},{7,6},{8,7},{9,8},{10,9},{11,1... | collective-permute-start | bytes 1179656 | tf_op jit(solution)/shard_map/ppermute | solution.py:30
  302.4 685.9 %reduce-scatter.17.cloned.1.call-start = ((), (), s32[]{:S(2)}) async-start(), calls=%async_computation.3 | async-start | bytes 2433024 | tf_op jit(solution)/shard_map/reduce_scatter | solution.py:104
  506.1 19.3 %collective-permute-start.4 = (bf16[256,768]{0,1:T(8,128)(2,1)}, bf16[256,768]{0,1:T(8,128)(2,1)}, u32[]{:S(2)}, u32[]{:S(2)}) collective-permute-start(bf16[256,768]{0,1:T(8,128)(2,1)} %get-tuple-element.771), channel_id=1, source_target_pairs={{1,0},{2,1},{3,2},{4,3},{5,4},{6,5},{7,6},{8,7},{9,8},{10,9},{11,1... | collective-permute-start | bytes 1179656 | tf_op jit(solution)/shard_map/ppermute | solution.py:19
  525.3 463.0 %reduce-scatter.15.cloned.1.call-start = ((), (), s32[]{:S(2)}) async-start(), calls=%async_computation.2 | async-start | bytes 2433024 | tf_op jit(solution)/shard_map/reduce_scatter | solution.py:104
  624.2 20.1 %collective-permute-start.6 = (bf16[256,768]{0,1:T(8,128)(2,1)}, bf16[256,768]{0,1:T(8,128)(2,1)}, u32[]{:S(2)}, u32[]{:S(2)}) collective-permute-start(bf16[256,768]{0,1:T(8,128)(2,1)} %get-tuple-element.769), channel_id=1, source_target_pairs={{1,0},{2,1},{3,2},{4,3},{5,4},{6,5},{7,6},{8,7},{9,8},{10,9},{11,1... | collective-permute-start | bytes 1179656 | tf_op jit(solution)/shard_map/ppermute | solution.py:19
  805.8 65.4 %collective-permute-start.38 = (f32[16,384]{1,0:T(8,128)S(1)}, f32[16,384]{1,0:T(8,128)S(1)}, u32[]{:S(2)}, u32[]{:S(2)}) collective-permute-start(f32[16,384]{1,0:T(8,128)S(1)} %get-tuple-element.730), channel_id=1, source_target_pairs={{0,7},{1,8},{2,9},{3,10},{4,11},{5,12},{6,13},{7,14},{8,15},{9,16}... | collective-permute-start | bytes 73736
  807.1 67.5 %collective-permute-start.37 = (f32[16,384]{1,0:T(8,128)S(1)}, f32[16,384]{1,0:T(8,128)S(1)}, u32[]{:S(2)}, u32[]{:S(2)}) collective-permute-start(f32[16,384]{1,0:T(8,128)S(1)} %get-tuple-element.730), channel_id=1, source_target_pairs={{0,6},{1,7},{2,8},{3,9},{4,10},{5,11},{6,12},{7,13},{8,14},{9,15},... | collective-permute-start | bytes 73736
  808.4 69.6 %collective-permute-start.36 = (f32[16,384]{1,0:T(8,128)S(1)}, f32[16,384]{1,0:T(8,128)S(1)}, u32[]{:S(2)}, u32[]{:S(2)}) collective-permute-start(f32[16,384]{1,0:T(8,128)S(1)} %get-tuple-element.730), channel_id=1, source_target_pairs={{0,5},{1,6},{2,7},{3,8},{4,9},{5,10},{6,11},{7,12},{8,13},{9,14},{... | collective-permute-start | bytes 73736
  809.8 55.7 %collective-permute-start.31 = (f32[12,384]{1,0:T(8,128)S(1)}, f32[12,384]{1,0:T(8,128)S(1)}, u32[]{:S(2)}, u32[]{:S(2)}) collective-permute-start(f32[12,384]{1,0:T(8,128)S(1)} %slice.358), channel_id=1, source_target_pairs={{0,8},{1,9},{2,10},{3,11},{4,12},{5,13},{6,14},{7,15},{8,16},{9,17... | collective-permute-start | bytes 55304
  813.1 55.0 %collective-permute-start.39 = (f32[12,384]{1,0:T(8,128)S(1)}, f32[12,384]{1,0:T(8,128)S(1)}, u32[]{:S(2)}, u32[]{:S(2)}) collective-permute-start(f32[12,384]{1,0:T(8,128)S(1)} %slice.359), channel_id=1, source_target_pairs={{0,8},{1,9},{2,10},{3,11},{4,12},{5,13},{6,14},{7,15},{8,16},{9,17... | collective-permute-start | bytes 55304
  892.1 16.6 %collective-permute-start.25 = (f32[16,384]{1,0:T(8,128)S(1)}, f32[16,384]{1,0:T(8,128)S(1)}, u32[]{:S(2)}, u32[]{:S(2)}) collective-permute-start(f32[16,384]{1,0:T(8,128)S(1)} %get-tuple-element.731), channel_id=1, source_target_pairs={{0,2},{1,3},{2,4},{3,5},{4,6},{5,7},{6,8},{7,9},{8,10},{9,11},{10,... | collective-permute-start | bytes 73736
  896.6 16.4 %collective-permute-start.15 = (f32[12,1152]{1,0:T(8,128)S(1)}, f32[12,1152]{1,0:T(8,128)S(1)}, u32[]{:S(2)}, u32[]{:S(2)}) collective-permute-start(f32[12,1152]{1,0:T(8,128)S(1)} %slice.356), channel_id=1, source_target_pairs={{0,8},{1,9},{2,10},{3,11},{4,12},{5,13},{6,14},{7,15},{8,16},{9,17... | collective-permute-start | bytes 165896
  898.2 17.0 %collective-permute-start.23 = (f32[12,1152]{1,0:T(8,128)S(1)}, f32[12,1152]{1,0:T(8,128)S(1)}, u32[]{:S(2)}, u32[]{:S(2)}) collective-permute-start(f32[12,1152]{1,0:T(8,128)S(1)} %slice.357), channel_id=1, source_target_pairs={{0,8},{1,9},{2,10},{3,11},{4,12},{5,13},{6,14},{7,15},{8,16},{9,17... | collective-permute-start | bytes 165896
  940.6 16.8 %collective-permute-start.54 = (f32[16,1536]{1,0:T(8,128)S(1)}, f32[16,1536]{1,0:T(8,128)S(1)}, u32[]{:S(2)}, u32[]{:S(2)}) collective-permute-start(f32[16,1536]{1,0:T(8,128)S(1)} %get-tuple-element.732), channel_id=1, source_target_pairs={{0,7},{1,8},{2,9},{3,10},{4,11},{5,12},{6,13},{7,14},{8,15},{9,16}... | collective-permute-start | bytes 294920
  942.8 17.6 %collective-permute-start.53 = (f32[16,1536]{1,0:T(8,128)S(1)}, f32[16,1536]{1,0:T(8,128)S(1)}, u32[]{:S(2)}, u32[]{:S(2)}) collective-permute-start(f32[16,1536]{1,0:T(8,128)S(1)} %get-tuple-element.732), channel_id=1, source_target_pairs={{0,6},{1,7},{2,8},{3,9},{4,10},{5,11},{6,12},{7,13},{8,14},{9,15},... | collective-permute-start | bytes 294920
  945.0 18.0 %collective-permute-start.52 = (f32[16,1536]{1,0:T(8,128)S(1)}, f32[16,1536]{1,0:T(8,128)S(1)}, u32[]{:S(2)}, u32[]{:S(2)}) collective-permute-start(f32[16,1536]{1,0:T(8,128)S(1)} %get-tuple-element.732), channel_id=1, source_target_pairs={{0,5},{1,6},{2,7},{3,8},{4,9},{5,10},{6,11},{7,12},{8,13},{9,14},{... | collective-permute-start | bytes 294920
  947.1 20.9 %collective-permute-start.51 = (f32[16,1536]{1,0:T(8,128)S(1)}, f32[16,1536]{1,0:T(8,128)S(1)}, u32[]{:S(2)}, u32[]{:S(2)}) collective-permute-start(f32[16,1536]{1,0:T(8,128)S(1)} %get-tuple-element.732), channel_id=1, source_target_pairs={{0,4},{1,5},{2,6},{3,7},{4,8},{5,9},{6,10},{7,11},{8,12},{9,13},{1... | collective-permute-start | bytes 294920
  (205 other events, 1928.5 us)
Sparse Core Ops, SparseCore 0:
  11.5 58.8 all-gather.28
  73.8 54.1 all-gather.30
  131.5 57.4 all-gather.32
  302.5 51.7 all-gather.34
  525.4 97.9 reduce-scatter.16
  644.4 105.6 reduce-scatter.14
where the time goes:
time: 1010 us; the launch traced here: 997 us
  blocking collectives  394 us (39%)
  matrix products  213 us (21%)
  starting transfers between devices  141 us (14%)
  local copies, waits for them, and re-layouts  112 us (11%)
  other arithmetic  105 us (10%)
  between operations  17.4 us (2%)
  waiting for transfers between devices  10.7 us (1%)
    unnamed x3, blocking collectives  227 us
    unnamed x48, starting transfers between devices  112 us
    all_gather x2, blocking collectives, fetch_forward(): lax.all_gather(shards[0], 'dev', axis=0, tiled=True)  87.5 us
    all_gather x2, blocking collectives, fetch_forward(): lax.all_gather(shards[2], 'dev', axis=0, tiled=True)  80.1 us
    dot_general x8, matrix products, product(): return jnp.dot(left, right, preferred_element_type=jnp.float32)  66.5 us
    dot_general x8, matrix products, contract_last(): lax.dot_general(left, right, (((1,), (1,)), ((), ())), preferred_element_...  33.1 us
    unnamed x303, local copies, waits for them, and re-layouts  31.2 us
    dot_general x4, matrix products, one_block(): jnp.einsum('qhd,khd->hqk', grad_block, value_heads, preferred_element_typ...  28.6 us
  transfers between devices with their start and end apart: 62, of which 5 were waited for; matrix products, arithmetic and copies ran while one was open for 47% of the time, Pallas kernels for 0%

commit v1 on v0

--- a/solution.py
+++ b/solution.py
@@ -61,7 +61,9 @@
 
 def fetch_forward(shards):
     return (
-        lax.all_gather(shards[0], "dev", axis=0, tiled=True),
+        jnp.concatenate(
+            lax.all_to_all(jnp.stack([shards[0]] * lax.axis_size("dev")), "dev", 0, 0), axis=0
+        ),
         lax.all_gather(shards[1], "dev", axis=0, tiled=True),
         lax.all_gather(shards[2], "dev", axis=0, tiled=True),
         lax.all_gather(shards[3], "dev", axis=0, tiled=True),

time: 1010 us -> 1110 us (1.099)
  matrix products: 213 us -> 245 us
  starting transfers between devices: 141 us -> 165 us
  other arithmetic: 105 us -> 124 us
  blocking collectives: 394 us -> 412 us
    dot_general x8, matrix products: 17 us -> 35.3 us  [block_scores(): jnp.einsum('qhd,khd->hqk', query_block, key_heads, preferred_element_type...]
    dot_general x4, matrix products: 28.6 us -> 45.3 us  [one_block(): jnp.einsum('qhd,khd->hqk', grad_block, value_heads, preferred_element_typ...]
    all_to_all x0 -> x2, starting transfers between devices: none -> 13 us  [fetch_forward(): lax.all_to_all(jnp.stack([shards[0]] * lax.axis_size('dev')), 'dev', 0, 0)]
    all_gather x2, blocking collectives: 87.5 us -> 98.9 us  [fetch_backward(): lax.all_gather(shards[0], 'dev', axis=0, tiled=True)]
    unnamed x303 -> x341, local copies, waits for them, and re-layouts: 31.2 us -> 28.2 us
  transfers between devices with their start and end apart: 62 -> 64, of which waited for: 5 -> 4; matrix products, arithmetic and copies ran while one was open for 47% -> 45% of each run, Pallas kernels for 0% -> 0%
where the time goes in v1:
time: 1110 us; the launch traced here: 1090 us
  blocking collectives  412 us (37%)
  matrix products  245 us (22%)
  starting transfers between devices  165 us (15%)
  other arithmetic  124 us (11%)
  local copies, waits for them, and re-layouts  113 us (10%)
  between operations  17.4 us (2%)
  waiting for transfers between devices  11.4 us (1%)
    unnamed x3, blocking collectives  231 us
    unnamed x48, starting transfers between devices  123 us
    all_gather x2, blocking collectives, fetch_backward(): lax.all_gather(shards[0], 'dev', axis=0, tiled=True)  98.9 us
    all_gather x2, blocking collectives, fetch_forward(): lax.all_gather(shards[2], 'dev', axis=0, tiled=True)  81.6 us
    dot_general x8, matrix products, product(): return jnp.dot(left, right, preferred_element_type=jnp.float32)  57 us
    dot_general x4, matrix products, one_block(): jnp.einsum('qhd,khd->hqk', grad_block, value_heads, preferred_element_typ...  45.3 us
    dot_general x8, matrix products, contract_last(): lax.dot_general(left, right, (((1,), (1,)), ((), ())), preferred_element_...  35.7 us
    dot_general x8, matrix products, block_scores(): jnp.einsum('qhd,khd->hqk', query_block, key_heads, preferred_element_type...  35.3 us
  transfers between devices with their start and end apart: 64, of which 4 were waited for; matrix products, arithmetic and copies ran while one was open for 45% of the time, Pallas kernels for 0%

profile of v1, /device:TPU:4, one launch (start us, length us, event | category | flops | bytes accessed | tf_op | source)
XLA Modules:
  0.0 1092.2 jit_solution(12618393640605026851)
XLA Ops:
  25.3 50.8 %all-reduce.45 = (bf16[768]{0:T(1024)(128)(2,1)}, bf16[768]{0:T(1024)(128)(2,1)}, bf16[384]{0:T(512)(128)(2,1)S(1)}, bf16[384]{0:T(512)(128)(2,1)S(1)}, bf16[384...) all-reduce(bf16[768]{0:T(1024)(128)(2,1)S(1)} %dynamic-update-slice, ...), channel_id=4, replica_groups=mesh['dev'=32] {'dev'}, use_global_device_ids=true, to_apply=%add.2 | all-reduce | flops 9216 | bytes 36864
  95.6 40.5 %all-gather.3 = bf16[1,384,384]{2,0,1:T(2,128)(2,1)} all-gather(bf16[1,12,384]{2,0,1:T(2,128)(2,1)S(1)} %get-tuple-element.784), channel_id=5, replica_groups=mesh['dev'=32] {'dev'}, dimensions={1}, use_global_device_ids=true | all-gather | bytes 304128 | tf_op jit(solution)/shard_map/all_gather | solution.py:68
  136.1 41.1 %all-gather.14 = bf16[1,384,384]{2,0,1:T(2,128)(2,1)} all-gather(bf16[1,12,384]{2,0,1:T(2,128)(2,1)S(1)} %get-tuple-element.783), channel_id=16, replica_groups=mesh['dev'=32] {'dev'}, dimensions={1}, use_global_device_ids=true | all-gather | bytes 304128 | tf_op jit(solution)/shard_map/all_gather | solution.py:68
  178.4 6.9 all-to-all-start.1
  198.5 54.7 %all-gather.22 = bf16[1,384,1152]{2,0,1:T(2,128)(2,1)} all-gather(bf16[1,12,1152]{2,0,1:T(2,128)(2,1)S(1)} %copy-done.59), channel_id=24, replica_groups=mesh['dev'=32] {'dev'}, dimensions={1}, use_global_device_ids=true | all-gather | bytes 912384 | tf_op jit(solution)/shard_map/all_gather | solution.py:83
  263.2 28.8 %while.58 = (s32[]{:T(128)}, bf16[2,512,384]{2,1,0:T(8,128)(2,1)}, f32[2,6,512]{2,1,0:T(8,128)S(1)}, s32[2]{0:T(128)S(1)}, bf16[1536,768]{0,1:T(8,128)(2,1)S(1)}...) while((s32[]{:T(128)}, bf16[2,512,384]{2,1,0:T(8,128)(2,1)}, ...), condition=%wide.region_5.6_spmd, body=%wide.region_2.5_spmd.sunk | while | flops 843772928 | bytes 50985752 | solution.py:153
  296.5 19.5 %multiply_convert_fusion.3 = (bf16[1024,1536]{1,0:T(8,128)(2,1)}, f32[1024,1536]{1,0:T(8,128)}, f32[1024,1536]{1,0:T(8,128)}) fusion(f32[1536]{0:T(1024)S(1)} %copy-done.119, bf16[1,384,1536]{2,0,1:T(2,128)(2,1)} %all-gather.29.cloned.1.call-done, f32[1024,384]{0,1:T(8,128)} %copy-done.18, f32[384]{0:T(512)S(1)} %copy-done.128, f32[384]{0:T(512)S(1)} %copy-done.102, ...), kind=kOutput, calls=%fused_computation.85 | convolution fusion | flops 1313734656 | bytes 18498560 | tf_op jit(solution)/shard_map/dot_general | solution.py:43
  330.8 44.2 %all-gather.23 = bf16[1,384,1152]{2,0,1:T(2,128)(2,1)} all-gather(bf16[1,12,1152]{2,0,1:T(2,128)(2,1)S(1)} %copy-done.58), channel_id=25, replica_groups=mesh['dev'=32] {'dev'}, dimensions={1}, use_global_device_ids=true | all-gather | bytes 912384 | tf_op jit(solution)/shard_map/all_gather | solution.py:83
  383.0 28.7 %while.59 = (s32[]{:T(128)}, bf16[2,512,384]{2,1,0:T(8,128)(2,1)}, f32[2,6,512]{2,1,0:T(8,128)S(1)}, s32[2]{0:T(128)S(1)}, bf16[1536,768]{0,1:T(8,128)(2,1)S(1)}...) while((s32[]{:T(128)}, bf16[2,512,384]{2,1,0:T(8,128)(2,1)}, ...), condition=%wide.region_13.14_spmd, body=%wide.region_10.13_spmd.sunk | while | flops 843772928 | bytes 50985752 | solution.py:153
  415.8 19.6 %multiply_convert_fusion.2 = (bf16[1024,1536]{1,0:T(8,128)(2,1)}, f32[1024,1536]{1,0:T(8,128)}, f32[1024,1536]{1,0:T(8,128)}) fusion(f32[1536]{0:T(1024)S(1)} %copy-done.121, bf16[1,384,1536]{2,0,1:T(2,128)(2,1)} %all-gather.33.cloned.1.call-done, f32[1024,384]{0,1:T(8,128)} %copy-done.21, f32[384]{0:T(512)S(1)} %copy-done.131, f32[384]{0:T(512)S(1)} %copy-done.107, ...), kind=kOutput, calls=%fused_computation.72 | convolution fusion | flops 1313734656 | bytes 18498560 | tf_op jit(solution)/shard_map/dot_general | solution.py:43
  435.4 7.8 convert_reduce_fusion
  460.3 85.7 %while.60 = (s32[]{:T(128)}, bf16[1024,384]{0,1:T(8,128)(2,1)}, f32[1536,768]{0,1:T(8,128)}, bf16[1536,768]{0,1:T(8,128)(2,1)S(1)}, s32[1024]{0:T(1024)S(1)}, /*...) while((s32[]{:T(128)}, bf16[1024,384]{0,1:T(8,128)(2,1)}, ...), condition=%wide.region_20.21_spmd, body=%wide.region_18.20_spmd.sunk | while | flops 2063332352 | bytes 199465520 | solution.py:205
  473.8 11.3 %multiply_reduce_fusion.13 = (f32[6,512]{1,0:T(8,128)S(1)}, f32[6,512,1024]{2,1,0:T(8,128)}) fusion(f32[6,512,1024]{2,1,0:T(8,128)} %fusion.253, f32[6,512]{1,0:T(8,128)S(1)} %dynamic-slice_bitcast_fusion.26, pred[512,1024]{1,0:T(8,128)(4,1)} %broadcast_compare_fusion.10, bf16[512,6,64]{0,2,1:T(8,128)(2,1)} %bitcast.370, ...), kind=kOutput, calls=%fused_computation.29.clone.1 | convolution fusion | flops 418378752 | bytes 26894336 | tf_op jit(solution)/shard_map/while/body/eval_jaxpr/qhd,khd->hqk/dot_general | solution.py:171
  485.2 6.9 multiply_convert_fusion.6
  516.5 11.3 %multiply_reduce_fusion.13 = (f32[6,512]{1,0:T(8,128)S(1)}, f32[6,512,1024]{2,1,0:T(8,128)}) fusion(f32[6,512,1024]{2,1,0:T(8,128)} %fusion.253, f32[6,512]{1,0:T(8,128)S(1)} %dynamic-slice_bitcast_fusion.26, pred[512,1024]{1,0:T(8,128)(4,1)} %broadcast_compare_fusion.10, bf16[512,6,64]{0,2,1:T(8,128)(2,1)} %bitcast.370, ...), kind=kOutput, calls=%fused_computation.29.clone.1 | convolution fusion | flops 418378752 | bytes 26894336 | tf_op jit(solution)/shard_map/while/body/eval_jaxpr/qhd,khd->hqk/dot_general | solution.py:171
  527.8 6.9 multiply_convert_fusion.6
  591.6 8.1 convert_reduce_fusion.1
  614.2 86.0 %while.61 = (s32[]{:T(128)}, bf16[1024,384]{0,1:T(8,128)(2,1)}, f32[1536,768]{0,1:T(8,128)}, bf16[1536,768]{0,1:T(8,128)(2,1)S(1)}, s32[1024]{0:T(1024)S(1)}, /*...) while((s32[]{:T(128)}, bf16[1024,384]{0,1:T(8,128)(2,1)}, ...), condition=%wide.region_27.28_spmd, body=%wide.region_25.27_spmd.sunk | while | flops 2063332352 | bytes 199465520 | solution.py:205
  627.9 11.4 %multiply_reduce_fusion.14 = (f32[6,512]{1,0:T(8,128)S(1)}, f32[6,512,1024]{2,1,0:T(8,128)}) fusion(f32[6,512,1024]{2,1,0:T(8,128)} %fusion.267, f32[6,512]{1,0:T(8,128)S(1)} %dynamic-slice_bitcast_fusion.27, pred[512,1024]{1,0:T(8,128)(4,1)} %broadcast_compare_fusion.11, bf16[512,6,64]{0,2,1:T(8,128)(2,1)} %bitcast.372, ...), kind=kOutput, calls=%fused_computation.47.clone.1 | convolution fusion | flops 418378752 | bytes 26894336 | tf_op jit(solution)/shard_map/while/body/eval_jaxpr/qhd,khd->hqk/dot_general | solution.py:171
  639.4 6.9 multiply_convert_fusion.7
  670.8 11.3 %multiply_reduce_fusion.14 = (f32[6,512]{1,0:T(8,128)S(1)}, f32[6,512,1024]{2,1,0:T(8,128)}) fusion(f32[6,512,1024]{2,1,0:T(8,128)} %fusion.267, f32[6,512]{1,0:T(8,128)S(1)} %dynamic-slice_bitcast_fusion.27, pred[512,1024]{1,0:T(8,128)(4,1)} %broadcast_compare_fusion.11, bf16[512,6,64]{0,2,1:T(8,128)(2,1)} %bitcast.372, ...), kind=kOutput, calls=%fused_computation.47.clone.1 | convolution fusion | flops 418378752 | bytes 26894336 | tf_op jit(solution)/shard_map/while/body/eval_jaxpr/qhd,khd->hqk/dot_general | solution.py:171
  682.1 6.9 multiply_convert_fusion.7
  742.5 140.9 %fusion.117 = (f32[16,1152]{1,0:T(8,128)}, f32[16,1152]{1,0:T(8,128)}, f32[16,384]{1,0:T(8,128)}, f32[16,384]{1,0:T(8,128)}, f32[16,1536]{1,0:T(8,128)}, /*index=5*/f32[16,1536]{1,0:T(8,128)}) fusion(f32[384,1152]{1,0:T(8,128)} %fusion.82, f32[384,1152]{1,0:T(8,128)} %fusion.81, f32[384,384]{1,0:T(8,128)S(1)} %copy-done.47, f32[384,384]{1,0:T(8,128)S(1)} %fusion.143, ...), kind=kCustom, calls=%all-reduce-scatter.6 | all-reduce-scatter fusion | flops 3145729 | bytes 9830400
  911.2 39.5 %all-reduce.44 = (f32[768]{0:T(1024)S(1)}, f32[768]{0:T(1024)S(1)}, f32[384]{0:T(512)S(1)}, f32[384]{0:T(512)S(1)}, f32[1536]{0:T(1024)S(1)}, /*index=5*/f32[153...) all-reduce(f32[768]{0:T(1024)S(1)} %pad_maximum_fusion.17, ...), channel_id=29, replica_groups=mesh['dev'=32] {'dev'}, use_global_device_ids=true, to_apply=%region_35.36.clone | all-reduce | flops 9216 | bytes 73728
  (828 shorter events, 524.1 us)
Async XLA Ops:
  7.3 289.2 %all-gather.29.cloned.1.call-start = ((), (), s32[]{:S(2)}) async-start(), calls=%async_computation.6 | async-start | bytes 2433024 | tf_op jit(solution)/shard_map/all_gather | solution.py:70
  9.1 307.0 %all-gather.31.cloned.1.call-start = ((), (), s32[]{:S(2)}) async-start(), calls=%async_computation.7 | async-start | bytes 1216512 | tf_op jit(solution)/shard_map/all_gather | solution.py:72
  10.7 405.0 %all-gather.33.cloned.1.call-start = ((), (), s32[]{:S(2)}) async-start(), calls=%async_computation.8 | async-start | bytes 2433024 | tf_op jit(solution)/shard_map/all_gather | solution.py:70
  14.8 162.6 %all-to-all-start = ((bf16[32,12,1152]{2,1,0:T(8,128)(2,1)}), bf16[32,12,1152]{2,1,0:T(8,128)(2,1)S(1)}, u32[]{:S(2)}, u32[]{:S(2)}) async-start(bf16[32,12,1152]{2,1,0:T(8,128)(2,1)} %stack.114), calls=%async_computation | async-start | bytes 2359296 | tf_op jit(solution)/shard_map/all_to_all | solution.py:65
  20.9 414.5 %all-gather.35.cloned.1.call-start = ((), (), s32[]{:S(2)}) async-start(), calls=%async_computation.9 | async-start | bytes 1216512 | tf_op jit(solution)/shard_map/all_gather | solution.py:72
  178.4 77.1 %all-to-all-start.1 = ((bf16[32,12,1152]{2,1,0:T(8,128)(2,1)}), bf16[32,12,1152]{2,1,0:T(8,128)(2,1)S(1)}, u32[]{:S(2)}, u32[]{:S(2)}) async-start(bf16[32,12,1152]{2,1,0:T(8,128)(2,1)} %stack.115), calls=%async_computation.1 | async-start | bytes 2359296 | tf_op jit(solution)/shard_map/all_to_all | solution.py:65
  185.4 897.9 %reduce-scatter.17.cloned.1.call-start = ((), (), s32[]{:S(2)}) async-start(), calls=%async_computation.5 | async-start | bytes 2433024 | tf_op jit(solution)/shard_map/reduce_scatter | solution.py:106
  192.0 64.6 %collective-permute-start = (bf16[256,768]{1,0:T(8,128)(2,1)}, bf16[256,768]{1,0:T(8,128)(2,1)S(1)}, u32[]{:S(2)}, u32[]{:S(2)}) collective-permute-start(bf16[256,768]{1,0:T(8,128)(2,1)} %get-tuple-element.774), channel_id=1, source_target_pairs={{0,1},{1,2},{2,3},{3,4},{4,5},{5,6},{6,7},{7,8},{8,9},{9,10},{10,1... | collective-permute-start | bytes 1179656 | tf_op jit(solution)/shard_map/ppermute | solution.py:27
  194.0 62.6 %collective-permute-start.1 = (bf16[256,768]{1,0:T(8,128)(2,1)}, bf16[256,768]{1,0:T(8,128)(2,1)}, u32[]{:S(2)}, u32[]{:S(2)}) collective-permute-start(bf16[256,768]{1,0:T(8,128)(2,1)} %get-tuple-element.775), channel_id=1, source_target_pairs={{1,0},{2,1},{3,2},{4,3},{5,4},{6,5},{7,6},{8,7},{9,8},{10,9},{11,1... | collective-permute-start | bytes 1179656 | tf_op jit(solution)/shard_map/ppermute | solution.py:30
  324.4 51.8 %collective-permute-start.2 = (bf16[256,768]{1,0:T(8,128)(2,1)}, bf16[256,768]{1,0:T(8,128)(2,1)S(1)}, u32[]{:S(2)}, u32[]{:S(2)}) collective-permute-start(bf16[256,768]{1,0:T(8,128)(2,1)} %get-tuple-element.772), channel_id=1, source_target_pairs={{0,1},{1,2},{2,3},{3,4},{4,5},{5,6},{6,7},{7,8},{8,9},{9,10},{10,1... | collective-permute-start | bytes 1179656 | tf_op jit(solution)/shard_map/ppermute | solution.py:27
  326.6 49.6 %collective-permute-start.3 = (bf16[256,768]{1,0:T(8,128)(2,1)S(1)}, bf16[256,768]{1,0:T(8,128)(2,1)}, u32[]{:S(2)}, u32[]{:S(2)}) collective-permute-start(bf16[256,768]{1,0:T(8,128)(2,1)S(1)} %get-tuple-element.773), channel_id=1, source_target_pairs={{1,0},{2,1},{3,2},{4,3},{5,4},{6,5},{7,6},{8,7},{9,8},{10,9},{11,1... | collective-permute-start | bytes 1179656 | tf_op jit(solution)/shard_map/ppermute | solution.py:30
  569.7 513.7 %reduce-scatter.15.cloned.1.call-start = ((), (), s32[]{:S(2)}) async-start(), calls=%async_computation.4 | async-start | bytes 2433024 | tf_op jit(solution)/shard_map/reduce_scatter | solution.py:106
  703.0 23.0 %collective-permute-start.6 = (bf16[256,768]{0,1:T(8,128)(2,1)S(1)}, bf16[256,768]{0,1:T(8,128)(2,1)}, u32[]{:S(2)}, u32[]{:S(2)}) collective-permute-start(bf16[256,768]{0,1:T(8,128)(2,1)S(1)} %get-tuple-element.769), channel_id=1, source_target_pairs={{1,0},{2,1},{3,2},{4,3},{5,4},{6,5},{7,6},{8,7},{9,8},{10,9},{11,1... | collective-permute-start | bytes 1179656 | tf_op jit(solution)/shard_map/ppermute | solution.py:19
  884.1 80.4 %collective-permute-start.24 = (f32[16,384]{1,0:T(8,128)}, f32[16,384]{1,0:T(8,128)S(1)}, u32[]{:S(2)}, u32[]{:S(2)}) collective-permute-start(f32[16,384]{1,0:T(8,128)} %get-tuple-element.731), channel_id=1, source_target_pairs={{0,1},{1,2},{2,3},{3,4},{4,5},{5,6},{6,7},{7,8},{8,9},{9,10},{10,1... | collective-permute-start | bytes 73736
  886.8 82.7 %collective-permute-start.25 = (f32[16,384]{1,0:T(8,128)}, f32[16,384]{1,0:T(8,128)S(1)}, u32[]{:S(2)}, u32[]{:S(2)}) collective-permute-start(f32[16,384]{1,0:T(8,128)} %get-tuple-element.731), channel_id=1, source_target_pairs={{0,2},{1,3},{2,4},{3,5},{4,6},{5,7},{6,8},{7,9},{8,10},{9,11},{10,... | collective-permute-start | bytes 73736
  891.0 81.3 %collective-permute-start.26 = (f32[16,384]{1,0:T(8,128)}, f32[16,384]{1,0:T(8,128)S(1)}, u32[]{:S(2)}, u32[]{:S(2)}) collective-permute-start(f32[16,384]{1,0:T(8,128)} %get-tuple-element.731), channel_id=1, source_target_pairs={{0,3},{1,4},{2,5},{3,6},{4,7},{5,8},{6,9},{7,10},{8,11},{9,12},{10... | collective-permute-start | bytes 73736
  905.1 53.5 %collective-permute-start.31 = (f32[12,384]{1,0:T(8,128)S(1)}, f32[12,384]{1,0:T(8,128)S(1)}, u32[]{:S(2)}, u32[]{:S(2)}) collective-permute-start(f32[12,384]{1,0:T(8,128)S(1)} %slice.364), channel_id=1, source_target_pairs={{0,8},{1,9},{2,10},{3,11},{4,12},{5,13},{6,14},{7,15},{8,16},{9,17... | collective-permute-start | bytes 55304
  906.4 55.2 %collective-permute-start.39 = (f32[12,384]{1,0:T(8,128)S(1)}, f32[12,384]{1,0:T(8,128)S(1)}, u32[]{:S(2)}, u32[]{:S(2)}) collective-permute-start(f32[12,384]{1,0:T(8,128)S(1)} %slice.365), channel_id=1, source_target_pairs={{0,8},{1,9},{2,10},{3,11},{4,12},{5,13},{6,14},{7,15},{8,16},{9,17... | collective-permute-start | bytes 55304
  997.0 19.1 %collective-permute-start.10 = (f32[16,1152]{1,0:T(8,128)S(1)}, f32[16,1152]{1,0:T(8,128)S(1)}, u32[]{:S(2)}, u32[]{:S(2)}) collective-permute-start(f32[16,1152]{1,0:T(8,128)S(1)} %copy-done.56), channel_id=1, source_target_pairs={{0,3},{1,4},{2,5},{3,6},{4,7},{5,8},{6,9},{7,10},{8,11},{9,12},{10... | collective-permute-start | bytes 221192
  998.9 19.1 %collective-permute-start.11 = (f32[16,1152]{1,0:T(8,128)S(1)}, f32[16,1152]{1,0:T(8,128)S(1)}, u32[]{:S(2)}, u32[]{:S(2)}) collective-permute-start(f32[16,1152]{1,0:T(8,128)S(1)} %copy-done.56), channel_id=1, source_target_pairs={{0,4},{1,5},{2,6},{3,7},{4,8},{5,9},{6,10},{7,11},{8,12},{9,13},{1... | collective-permute-start | bytes 221192
  1002.7 18.3 %collective-permute-start.12 = (f32[16,1152]{1,0:T(8,128)S(1)}, f32[16,1152]{1,0:T(8,128)S(1)}, u32[]{:S(2)}, u32[]{:S(2)}) collective-permute-start(f32[16,1152]{1,0:T(8,128)S(1)} %copy-done.56), channel_id=1, source_target_pairs={{0,5},{1,6},{2,7},{3,8},{4,9},{5,10},{6,11},{7,12},{8,13},{9,14},{... | collective-permute-start | bytes 221192
  1005.4 19.2 %collective-permute-start.13 = (f32[16,1152]{1,0:T(8,128)S(1)}, f32[16,1152]{1,0:T(8,128)S(1)}, u32[]{:S(2)}, u32[]{:S(2)}) collective-permute-start(f32[16,1152]{1,0:T(8,128)S(1)} %copy-done.56), channel_id=1, source_target_pairs={{0,6},{1,7},{2,8},{3,9},{4,10},{5,11},{6,12},{7,13},{8,14},{9,15},... | collective-permute-start | bytes 221192
  1040.9 19.7 %collective-permute-start.41 = (f32[16,1536]{1,0:T(8,128)S(1)}, f32[16,1536]{1,0:T(8,128)S(1)}, u32[]{:S(2)}, u32[]{:S(2)}) collective-permute-start(f32[16,1536]{1,0:T(8,128)S(1)} %copy-done.50), channel_id=1, source_target_pairs={{0,2},{1,3},{2,4},{3,5},{4,6},{5,7},{6,8},{7,9},{8,10},{9,11},{10,... | collective-permute-start | bytes 294920
  1043.9 18.1 %collective-permute-start.42 = (f32[16,1536]{1,0:T(8,128)S(1)}, f32[16,1536]{1,0:T(8,128)S(1)}, u32[]{:S(2)}, u32[]{:S(2)}) collective-permute-start(f32[16,1536]{1,0:T(8,128)S(1)} %copy-done.50), channel_id=1, source_target_pairs={{0,3},{1,4},{2,5},{3,6},{4,7},{5,8},{6,9},{7,10},{8,11},{9,12},{10... | collective-permute-start | bytes 294920
  (225 other events, 2427.4 us)
Sparse Core Ops, SparseCore 0:
  11.6 63.6 all-gather.28
  78.2 53.0 all-gather.30
  134.8 56.6 all-gather.32
  194.8 56.6 all-gather.34
  569.8 97.9 reduce-scatter.16
  726.2 104.7 reduce-scatter.14
